TPU v7x, 256 devices: a whole 4x4x8 slice. The times are simulated.
256 devices in a mesh: rows: 64 (over x, z, core), cols: 4 (over y).
Axes of the slice: x: 4, y: 4, z: 8, core: 2. Of those that a mesh axis runs over, the one named last changes fastest.
Arguments:
- column_lists: int32 [256, 13], replicated, may hold values from -1 to 255, as said below
- block_values: bfloat16 [256, 13, 128, 128], P('rows'), as said below
Outputs:
- purified: bfloat16 [256, 13, 128, 128], P('rows', None, None, 'cols')
Inputs may be any that keep to these rules, and one draw needn't show every extreme that they name: `column_lists`: slot (13 - 1) // 2 of row i holds i. Slot s of row i holds -1 or a row j, and then slot 12 - s of row j holds i. There is an ordering of the rows, taken cyclically, in which the row in slot s of row i stands s - (13 - 1) // 2 places after row i. With owners the aligned groups of 4 rows, the slots of one owner's rows hold at most 2 rows of any one other owner, and some pair of owners has exactly 2. Over the slots s of one owner's rows that hold rows of one other owner, the sum of 13 - |s - (13 - 1) // 2| is at most 16, and exactly 16 for some pair of owners. block_values[j, 12 - s] is the transpose of block_values[i, s] where slot s of row i holds j; blocks of empty slots are zero.
All inputs are finite; a program needn't handle non-finite values.
Results may differ from a plain program's by a relative error of at most 0.0039.
Values may be sent and summed in bfloat16 or wider, within the bound.
No kernel may reach another device: no remote copies, remote signals or barrier semaphores. Data moves between devices by JAX's collectives and lax.ppermute only.
A program may use at most 128 MiB of HBM per device.

v0:
```python
import jax
import jax.numpy as jnp
from jax import lax
from jax.sharding import PartitionSpec as P

CAP = 2


def body(column_lists, block_values):
    rows_here = block_values.shape[0]
    slot_count = block_values.shape[1]
    block_size = block_values.shape[2]
    middle = (slot_count - 1) // 2
    owners = lax.axis_size("rows")
    strip_width = block_size // lax.axis_size("cols")
    row_index = lax.axis_index("rows")
    column_part = lax.axis_index("cols")
    all_rows = column_lists.shape[0]
    present = column_lists >= 0
    target = jnp.maximum(column_lists, 0)
    owner_of = target // rows_here
    home_owner = (jnp.arange(all_rows, dtype=jnp.int32) // rows_here)[:, None]
    crossing = present & (owner_of != home_owner)
    dest_hot = (
        crossing[:, :, None] & (owner_of[:, :, None] == jnp.arange(owners, dtype=jnp.int32))
    ).astype(jnp.int32)
    first_row = row_index * rows_here
    own_present = lax.dynamic_slice_in_dim(present, first_row, rows_here, 0)
    my_cross = lax.dynamic_slice_in_dim(crossing, first_row, rows_here, 0)
    my_owner = lax.dynamic_slice_in_dim(owner_of, first_row, rows_here, 0)
    my_target = lax.dynamic_slice_in_dim(target, first_row, rows_here, 0)
    full_rows = jnp.where(
        own_present[:, :, None, None], block_values, jnp.zeros((), block_values.dtype)
    )
    own_strip = lax.dynamic_slice_in_dim(full_rows, column_part * strip_width, strip_width, 3)
    slot_ids = jnp.arange(slot_count, dtype=jnp.int32)
    running = jnp.cumsum(dest_hot.reshape(owners, rows_here * slot_count, owners), axis=1)
    running = running.reshape(all_rows, slot_count, owners)
    ranking = jnp.sum(running * dest_hot, axis=2) - 1
    my_rank = lax.dynamic_slice_in_dim(ranking, first_row, rows_here, 0)
    filler = jnp.zeros((1, slot_count - 1, block_size, strip_width), own_strip.dtype)
    local_stack = jnp.concatenate([own_strip[:, : slot_count - 1], own_strip[:, 1:], filler], 0)
    zero_entry = 2 * rows_here
    slot_of = jnp.where(my_cross, my_owner * CAP + my_rank, owners * CAP)
    stack_entry = (
        jnp.arange(rows_here, dtype=jnp.int32)[:, None]
        + jnp.where(slot_ids < middle, 0, rows_here)[None, :]
    )
    source = jnp.full((owners * CAP + 1,), zero_entry, jnp.int32)
    source = source.at[slot_of.reshape(-1)].set(stack_entry.reshape(-1))[: owners * CAP]
    outgoing = local_stack[source]
    back_rank = ranking[my_target, (slot_count - 1 - slot_ids)[None, :]]
    local_pick = (
        owners * CAP + my_target - first_row + jnp.where(slot_ids > middle, 0, rows_here)[None, :]
    )
    remote_pick = my_owner * CAP + back_rank
    empty_entry = owners * CAP + zero_entry
    table_pick = jnp.where(
        own_present & (my_owner == row_index),
        local_pick,
        jnp.where(own_present, remote_pick, empty_entry),
    )
    table_pick = table_pick.at[:, middle].set(empty_entry)
    arrived = lax.all_to_all(outgoing, "rows", split_axis=0, concat_axis=0, tiled=True)
    lookup = jnp.concatenate([arrived, local_stack], 0)
    picked = lookup[table_pick]
    by_slot = []
    for slot_index in range(slot_count):
        offset = slot_index - middle
        if offset == 0:
            by_slot.append(own_strip)
        elif offset > 0:
            by_slot.append(
                jnp.pad(
                    picked[:, slot_index, : slot_count - offset],
                    ((0, 0), (offset, 0), (0, 0), (0, 0)),
                )
            )
        else:
            by_slot.append(
                jnp.pad(
                    picked[:, slot_index, -offset - 1 :], ((0, 0), (0, -offset), (0, 0), (0, 0))
                )
            )
    windows = jnp.stack(by_slot, 1)
    square_sum = jnp.einsum(
        "iapq,iasqc->ispc", full_rows, windows, preferred_element_type=jnp.float32
    )
    square = jnp.where(own_present[:, :, None, None], square_sum, 0.0).astype(jnp.bfloat16)
    cube_sum = jnp.einsum(
        "iapq,iasqc->ispc",
        lax.all_gather(square, "cols", axis=3, tiled=True),
        windows,
        preferred_element_type=jnp.float32,
    )
    purified = jnp.where(
        own_present[:, :, None, None], 3.0 * square.astype(jnp.float32) - 2.0 * cube_sum, 0.0
    )
    return purified.astype(jnp.bfloat16)


def solution(mesh):
    in_specs = (P(), P("rows", None, None, None))
    out_specs = P("rows", None, None, "cols")
    return jax.shard_map(body, mesh=mesh, in_specs=in_specs, out_specs=out_specs, check_vma=False)
```

profile of v0, /device:TPU:1, one launch (start us, length us, event | category | flops | bytes accessed | tf_op | source)
XLA Modules:
  0.0 390.3 jit_solution(5772552660954711740)
XLA Ops:
  6.6 0.8 copy.54
  8.1 2.7 select_reduce_fusion
  11.0 1.0 gather_fusion.1
  12.1 2.8 copy.55
  15.1 0.7 scatter_custom_fusion
  16.2 1.1 copy-done
  17.6 8.0 %gather_fusion = bf16[128,12,128,32]{2,3,1,0:T(8,128)(2,1)} fusion(bf16[9,12,128,32]{2,3,1,0:T(8,128)(2,1)S(1)} %pad_maximum_fusion.1, s32[1024]{0:T(1024)S(1)} %pad_clamp_fusion.1), kind=kCustom, calls=%fused_computation | custom fusion | bytes 25166336 | tf_op jit(solution)/shard_map/gather | solution.py:51
  25.7 13.3 %all-to-all-start = ((bf16[128,12,128,32]{2,3,1,0:T(8,128)(2,1)}), bf16[128,12,128,32]{2,3,1,0:T(8,128)(2,1)}, u32[]{:S(2)}, u32[]{:S(2)}) async-start(bf16[128,12,128,32]{2,3,1,0:T(8,128)(2,1)} %gather_fusion), calls=%async_computation | async-start | bytes 25165824 | tf_op jit(solution)/shard_map/all_to_all | solution.py:64
  39.0 0.7 compare_reduce_fusion
  39.7 0.8 slice_select_fusion
  40.8 273.8 %all-to-all-done = bf16[128,12,128,32]{2,3,1,0:T(8,128)(2,1)} async-done(((bf16[128,12,128,32]{2,3,1,0:T(8,128)(2,1)}), bf16[128,12,128,32]{2,3,1,0:T(8,128)(2,1)}, u32[]{:S(2)}, u32[]{:S(2)}) %all-to-all-start) | async-done | bytes 12582944 | tf_op jit(solution)/shard_map/all_to_all | solution.py:64
  314.6 14.4 %pad_maximum_fusion = bf16[137,12,128,32]{2,3,1,0:T(8,128)(2,1)} fusion(bf16[1,12,128,32]{2,3,1,0:T(8,128)(2,1)S(1)} %broadcast_in_dim.85, bf16[4,12,128,32]{2,3,1,0:T(8,128)(2,1)S(1)} %copy-done.4, bf16[4,12,128,32]{2,3,1,0:T(8,128)(2,1)S(1)} %copy-done.2, bf16[128,12,128,32]{2,3,1,0:T(8,128)(2,1)} %all-to-all-done), kind=kLoop, calls=%fused_computation.4 | loop fusion | flops 20201472 | bytes 26935296 | tf_op jit(solution)/shard_map/concatenate | solution.py:65
  329.0 8.4 %gather_fusion.2 = bf16[52,12,128,32]{2,3,1,0:T(8,128)(2,1)} fusion(bf16[137,12,128,32]{2,3,1,0:T(8,128)(2,1)} %pad_maximum_fusion, s32[1024]{0:T(1024)S(1)} %pad_clamp_fusion), kind=kCustom, calls=%fused_computation.2 | custom fusion | bytes 10223824 | tf_op jit(solution)/shard_map/gather | solution.py:66
  337.4 1.1 slice_bitcast_fusion.10
  338.4 1.1 slice_bitcast_fusion.8
  339.5 1.1 slice_bitcast_fusion.6
  340.6 1.1 slice_bitcast_fusion.4
  341.7 1.1 slice_bitcast_fusion.2
  342.9 1.2 slice_bitcast_fusion
  344.5 1.1 bitcast_dynamic-update-slice_fusion.6
  346.1 2.4 copy-done.5
  348.5 2.4 fusion.35
  350.9 27.1 %all-gather.2.cloned.1.call-done = bf16[4,13,128,128]{2,3,1,0:T(8,128)(2,1)} async-done(((bf16[4,13,128,32]{2,3,1,0:T(8,128)(2,1)}), bf16[4,13,128,128]{2,3,1,0:T(8,128)(2,1)}) %all-gather.2.cloned.1.call-update) | async-done | bytes 1703952 | tf_op jit(solution)/shard_map/all_gather | solution.py:92
  378.0 5.4 %fusion.26 = bf16[4,13,128,32]{2,3,1,0:T(8,128)(2,1)} fusion(bf16[4,13,13,128,32]{3,4,1,2,0:T(8,128)(2,1)} %copy-done.5, bf16[4,13,128,128]{2,3,1,0:T(8,128)(2,1)} %all-gather.2.cloned.1.call-done, bf16[4,13,128,32]{2,3,1,0:T(8,128)(2,1)} %fusion.35, pred[4,13]{1,0:T(4,128)(4,1)S(1)} %get-tuple-element.18), kind=kOutput, calls=%fused_computation.21 | convolution fusion | flops 710115328 | bytes 8093748 | tf_op jit(solution)/shard_map/iapq,iasqc->ispc/dot_general | solution.py:90
  (54 shorter events, 3.0 us)
Async XLA Ops:
  16.1 1.2 copy-start
  16.2 1.2 copy-start.1
  16.2 1.3 copy-start.3
  25.7 288.9 %copy-start.2 = (bf16[4,12,128,32]{2,3,1,0:T(8,128)(2,1)S(1)}, bf16[4,12,128,32]{2,3,1,0:T(8,128)(2,1)}, u32[]{:S(2)}) copy-start(bf16[4,12,128,32]{2,3,1,0:T(8,128)(2,1)} %copy-done.1) | copy-start | bytes 1179652
  25.7 288.9 %copy-start.4 = (bf16[4,12,128,32]{2,3,1,0:T(8,128)(2,1)S(1)}, bf16[4,12,128,32]{2,3,1,0:T(8,128)(2,1)}, u32[]{:S(2)}) copy-start(bf16[4,12,128,32]{2,3,1,0:T(8,128)(2,1)} %copy-done.3) | copy-start | bytes 1179652
  25.7 288.9 %all-to-all-start = ((bf16[128,12,128,32]{2,3,1,0:T(8,128)(2,1)}), bf16[128,12,128,32]{2,3,1,0:T(8,128)(2,1)}, u32[]{:S(2)}, u32[]{:S(2)}) async-start(bf16[128,12,128,32]{2,3,1,0:T(8,128)(2,1)} %gather_fusion), calls=%async_computation | async-start | bytes 25165824 | tf_op jit(solution)/shard_map/all_to_all | solution.py:64
  38.9 339.1 %all-gather.2.cloned.1.call-start = ((), (), s32[]{:S(2)}) async-start(), calls=%async_computation.1 | async-start | bytes 2129920 | tf_op jit(solution)/shard_map/all_gather | solution.py:92
  346.1 2.4 copy-start.5
Sparse Core Ops, SparseCore 0:
  351.0 26.9 all-gather.1
where the time goes:
time: 391 us; the launch traced here: 390 us
  waiting for transfers between devices  301 us (77%)
  local copies, waits for them, and re-layouts  35.4 us (9%)
  other arithmetic  19.1 us (5%)
  between operations  13.7 us (4%)
  starting transfers between devices  13.3 us (3%)
  matrix products  7.86 us (2%)
    all_to_all x1, waiting for transfers between devices, body(): lax.all_to_all(outgoing, 'rows', split_axis=0, concat_axis=0, tiled=True)  274 us
    all_gather x1, waiting for transfers between devices, body(): lax.all_gather(square, 'cols', axis=3, tiled=True)  27.1 us
    concatenate x1, other arithmetic, body(): lookup = jnp.concatenate([arrived, local_stack], 0)  14.4 us
    all_to_all x1, starting transfers between devices, body(): lax.all_to_all(outgoing, 'rows', split_axis=0, concat_axis=0, tiled=True)  13.3 us
    unnamed x26, local copies, waits for them, and re-layouts  9.2 us
    gather x1, local copies, waits for them, and re-layouts, body(): picked = lookup[table_pick]  8.37 us
    gather x1, local copies, waits for them, and re-layouts, body(): outgoing = local_stack[source]  8.05 us
  transfers between devices with their start and end apart: 2, of which 2 were waited for; matrix products, arithmetic and copies ran while one was open for 0% of the time, Pallas kernels for 0%

commit v1 on v0

--- a/solution.py
+++ b/solution.py
@@ -4,6 +4,24 @@
 from jax.sharding import PartitionSpec as P
 
 CAP = 2
+
+
+def gather_around(array, axis, dim):
+    ways, here, turn = (lax.axis_size(axis), lax.axis_index(axis), array.shape[dim])
+    shape = [n * ways if d == dim else n for d, n in enumerate(array.shape)]
+    full = lax.dynamic_update_slice_in_dim(
+        jnp.zeros(shape, array.dtype), array, here * turn, axis=dim
+    )
+    going_up = going_down = array
+    for far in range(1, ways // 2 + 1):
+        going_up = lax.ppermute(going_up, axis, [(d, (d + 1) % ways) for d in range(ways)])
+        full = lax.dynamic_update_slice_in_dim(full, going_up, (here - far) % ways * turn, axis=dim)
+        if 2 * far < ways:
+            going_down = lax.ppermute(going_down, axis, [(d, (d - 1) % ways) for d in range(ways)])
+            full = lax.dynamic_update_slice_in_dim(
+                full, going_down, (here + far) % ways * turn, axis=dim
+            )
+    return full
 
 
 def body(column_lists, block_values):
@@ -89,7 +107,7 @@
     square = jnp.where(own_present[:, :, None, None], square_sum, 0.0).astype(jnp.bfloat16)
     cube_sum = jnp.einsum(
         "iapq,iasqc->ispc",
-        lax.all_gather(square, "cols", axis=3, tiled=True),
+        gather_around(square, "cols", 3),
         windows,
         preferred_element_type=jnp.float32,
     )

time: 391 us -> 374 us (0.957)
  between operations: 13.7 us -> 0.37 us
  waiting for transfers between devices: 301 us -> 297 us
    all_gather x1 -> x0, waiting for transfers between devices: 27.1 us -> none  [body(): lax.all_gather(square, 'cols', axis=3, tiled=True)]
    ppermute x0 -> x3, waiting for transfers between devices: none -> 22.6 us  [the longest x2 22.6 us: gather_around(): lax.ppermute(going_up, axis, [(d, (d + 1) % ways) for d in range(ways)])]
  transfers between devices with their start and end apart: 2 -> 4, of which waited for: 2 -> 3; matrix products, arithmetic and copies ran while one was open for 0% -> 0% of each run, Pallas kernels for 0% -> 0%
where the time goes in v1:
time: 374 us; the launch traced here: 373 us
  waiting for transfers between devices  297 us (79%)
  local copies, waits for them, and re-layouts  33.5 us (9%)
  other arithmetic  19.1 us (5%)
  starting transfers between devices  16 us (4%)
  matrix products  7.58 us (2%)
    all_to_all x1, waiting for transfers between devices, body(): lax.all_to_all(outgoing, 'rows', split_axis=0, concat_axis=0, tiled=True)  274 us
    ppermute x2, waiting for transfers between devices, gather_around(): lax.ppermute(going_up, axis, [(d, (d + 1) % ways) for d in range(ways)])  22.6 us
    concatenate x1, other arithmetic, body(): lookup = jnp.concatenate([arrived, local_stack], 0)  14.4 us
    all_to_all x1, starting transfers between devices, body(): lax.all_to_all(outgoing, 'rows', split_axis=0, concat_axis=0, tiled=True)  13.3 us
    gather x1, local copies, waits for them, and re-layouts, body(): picked = lookup[table_pick]  8.38 us
    gather x1, local copies, waits for them, and re-layouts, body(): outgoing = local_stack[source]  8.04 us
  transfers between devices with their start and end apart: 4, of which 3 were waited for; matrix products, arithmetic and copies ran while one was open for 0% of the time, Pallas kernels for 0%

profile of v1, /device:TPU:1, one launch (start us, length us, event | category | flops | bytes accessed | tf_op | source)
XLA Modules:
  0.0 373.1 jit_solution(13799417877230735728)
XLA Ops:
  0.0 0.8 copy.63
  1.6 2.7 select_reduce_fusion
  4.5 1.0 gather_fusion.1
  5.5 2.8 copy.64
  8.6 0.7 scatter_custom_fusion
  9.7 1.1 copy-done
  11.1 8.0 %gather_fusion = bf16[128,12,128,32]{2,3,1,0:T(8,128)(2,1)} fusion(bf16[9,12,128,32]{2,3,1,0:T(8,128)(2,1)S(1)} %pad_maximum_fusion.1, s32[1024]{0:T(1024)S(1)} %pad_clamp_fusion.1), kind=kCustom, calls=%fused_computation | custom fusion | bytes 25166336 | tf_op jit(solution)/shard_map/gather | solution.py:69
  19.1 13.3 %all-to-all-start = ((bf16[128,12,128,32]{2,3,1,0:T(8,128)(2,1)}), bf16[128,12,128,32]{2,3,1,0:T(8,128)(2,1)}, u32[]{:S(2)}, u32[]{:S(2)}) async-start(bf16[128,12,128,32]{2,3,1,0:T(8,128)(2,1)} %gather_fusion), calls=%async_computation | async-start | bytes 25165824 | tf_op jit(solution)/shard_map/all_to_all | solution.py:82
  34.1 274.0 %all-to-all-done = bf16[128,12,128,32]{2,3,1,0:T(8,128)(2,1)} async-done(((bf16[128,12,128,32]{2,3,1,0:T(8,128)(2,1)}), bf16[128,12,128,32]{2,3,1,0:T(8,128)(2,1)}, u32[]{:S(2)}, u32[]{:S(2)}) %all-to-all-start) | async-done | bytes 12582944 | tf_op jit(solution)/shard_map/all_to_all | solution.py:82
  308.1 14.4 %pad_maximum_fusion = bf16[137,12,128,32]{2,3,1,0:T(8,128)(2,1)} fusion(bf16[1,12,128,32]{2,3,1,0:T(8,128)(2,1)S(1)} %broadcast_in_dim.86, bf16[4,12,128,32]{2,3,1,0:T(8,128)(2,1)S(1)} %copy-done.4, bf16[4,12,128,32]{2,3,1,0:T(8,128)(2,1)S(1)} %copy-done.2, bf16[128,12,128,32]{2,3,1,0:T(8,128)(2,1)} %all-to-all-done), kind=kLoop, calls=%fused_computation.4 | loop fusion | flops 20201472 | bytes 26935296 | tf_op jit(solution)/shard_map/concatenate | solution.py:83
  322.5 8.4 %gather_fusion.2 = bf16[52,12,128,32]{2,3,1,0:T(8,128)(2,1)} fusion(bf16[137,12,128,32]{2,3,1,0:T(8,128)(2,1)} %pad_maximum_fusion, s32[1024]{0:T(1024)S(1)} %pad_clamp_fusion), kind=kCustom, calls=%fused_computation.2 | custom fusion | bytes 10223824 | tf_op jit(solution)/shard_map/gather | solution.py:84
  330.8 1.1 slice_bitcast_fusion.10
  331.9 1.1 slice_bitcast_fusion.8
  333.0 1.1 slice_bitcast_fusion.6
  334.1 1.1 slice_bitcast_fusion.4
  335.2 1.1 slice_bitcast_fusion.2
  336.4 1.2 slice_bitcast_fusion
  338.0 1.1 bitcast_dynamic-update-slice_fusion.6
  340.0 2.6 constant_dynamic-update-slice_fusion.3
  342.6 1.3 collective-permute-start
  343.9 1.4 collective-permute-start.1
  345.3 10.5 %collective-permute-done = bf16[4,13,128,32]{2,3,1,0:T(8,128)(2,1)S(1)} collective-permute-done((bf16[4,13,128,32]{2,3,1,0:T(8,128)(2,1)}, bf16[4,13,128,32]{2,3,1,0:T(8,128)(2,1)S(1)}, u32[]{:S(2)}, u32[]{:S(2)}) %collective-permute-start) | collective-permute-done | bytes 426016 | tf_op jit(solution)/shard_map/ppermute | solution.py:17
  356.0 12.0 %collective-permute-done.2 = bf16[4,13,128,32]{2,3,1,0:T(8,128)(2,1)S(1)} collective-permute-done((bf16[4,13,128,32]{2,3,1,0:T(8,128)(2,1)S(1)}, bf16[4,13,128,32]{2,3,1,0:T(8,128)(2,1)S(1)}, u32[]{:S(2)}, u32[]{:S(2)}) %collective-permute-start.2) | collective-permute-done | bytes 426016 | tf_op jit(solution)/shard_map/ppermute | solution.py:17
  368.1 5.0 %fusion.26 = bf16[4,13,128,32]{2,3,1,0:T(8,128)(2,1)} fusion(bf16[4,13,13,128,32]{3,4,1,2,0:T(8,128)(2,1)} %copy-done.5, bf16[4,13,128,128]{2,3,1,0:T(8,128)(2,1)S(1)} %constant_dynamic-update-slice_fusion, bf16[4,13,128,32]{2,3,1,0:T(8,128)(2,1)} %get-tuple-element.39, pred[4,13]{1,0:T(4,128)(4,1)S(1)} %get-tuple-element.18), kind=kOutput, calls=%fused_computation.21 | convolution fusion | flops 710115328 | bytes 8093748 | tf_op jit(solution)/shard_map/iapq,iasqc->ispc/dot_general | solution.py:108
  (61 shorter events, 4.9 us)
Async XLA Ops:
  9.5 1.2 copy-start
  9.7 1.2 copy-start.1
  9.7 1.3 copy-start.3
  19.1 288.9 %copy-start.2 = (bf16[4,12,128,32]{2,3,1,0:T(8,128)(2,1)S(1)}, bf16[4,12,128,32]{2,3,1,0:T(8,128)(2,1)}, u32[]{:S(2)}) copy-start(bf16[4,12,128,32]{2,3,1,0:T(8,128)(2,1)} %copy-done.1) | copy-start | bytes 1179652
  19.1 288.9 %copy-start.4 = (bf16[4,12,128,32]{2,3,1,0:T(8,128)(2,1)S(1)}, bf16[4,12,128,32]{2,3,1,0:T(8,128)(2,1)}, u32[]{:S(2)}) copy-start(bf16[4,12,128,32]{2,3,1,0:T(8,128)(2,1)} %copy-done.3) | copy-start | bytes 1179652
  19.1 288.9 %all-to-all-start = ((bf16[128,12,128,32]{2,3,1,0:T(8,128)(2,1)}), bf16[128,12,128,32]{2,3,1,0:T(8,128)(2,1)}, u32[]{:S(2)}, u32[]{:S(2)}) async-start(bf16[128,12,128,32]{2,3,1,0:T(8,128)(2,1)} %gather_fusion), calls=%async_computation | async-start | bytes 25165824 | tf_op jit(solution)/shard_map/all_to_all | solution.py:82
  339.6 3.0 copy-start.5
  342.6 13.3 %collective-permute-start = (bf16[4,13,128,32]{2,3,1,0:T(8,128)(2,1)}, bf16[4,13,128,32]{2,3,1,0:T(8,128)(2,1)S(1)}, u32[]{:S(2)}, u32[]{:S(2)}) collective-permute-start(bf16[4,13,128,32]{2,3,1,0:T(8,128)(2,1)} %get-tuple-element.39), channel_id=1, source_target_pairs={{0,1},{1,2},{2,3},{3,0},{4,5},{5,6},{6,7},{7,4},{8,9},{9,10},{10,1... | collective-permute-start | bytes 1277960 | tf_op jit(solution)/shard_map/ppermute | solution.py:17
  343.9 12.1 %collective-permute-start.1 = (bf16[4,13,128,32]{2,3,1,0:T(8,128)(2,1)}, bf16[4,13,128,32]{2,3,1,0:T(8,128)(2,1)S(1)}, u32[]{:S(2)}, u32[]{:S(2)}) collective-permute-start(bf16[4,13,128,32]{2,3,1,0:T(8,128)(2,1)} %get-tuple-element.39), channel_id=1, source_target_pairs={{0,3},{1,0},{2,1},{3,2},{4,7},{5,4},{6,5},{7,6},{8,11},{9,8},{10,9... | collective-permute-start | bytes 1277960 | tf_op jit(solution)/shard_map/ppermute | solution.py:20
  355.8 12.2 %collective-permute-start.2 = (bf16[4,13,128,32]{2,3,1,0:T(8,128)(2,1)S(1)}, bf16[4,13,128,32]{2,3,1,0:T(8,128)(2,1)S(1)}, u32[]{:S(2)}, u32[]{:S(2)}) collective-permute-start(bf16[4,13,128,32]{2,3,1,0:T(8,128)(2,1)S(1)} %collective-permute-done), channel_id=1, source_target_pairs={{0,1},{1,2},{2,3},{3,0},{4,5},{5,6},{6,7},{7,4},{8,9},{9,10},{10,1... | collective-permute-start | bytes 1277960 | tf_op jit(solution)/shard_map/ppermute | solution.py:17
